TPU v7x, 32 devices: a whole 2x2x4 slice. The times are simulated.
32 devices in a mesh: pb: 4 (over x, core), ga: 8 (over z, y).
Axes of the slice: x: 2, y: 2, z: 4, core: 2. Of those that a mesh axis runs over, the one named last changes fastest.
Arguments:
- queries: bfloat16 [8192, 512], P(('pb', 'ga')), may hold values from -4 to 4
- gallery: bfloat16 [12288, 512], P('ga'), may hold values from -1 to 1
- positives: int32 [8192, 4], P('pb'), may hold values from 0 to 12287, as said below
- cutoffs: int32 [4], replicated, may hold values from 1 to 385
Outputs:
- query_grad: float32 [8192, 512], P(('pb', 'ga'))
- gallery_grad: float32 [12288, 512], P(('ga', 'pb'))
Inputs may be any that keep to these rules, and one draw needn't show every extreme that they name: `positives`: indices of a query may repeat.
All inputs are finite; a program needn't handle non-finite values.
Results may differ from a plain program's by a relative error of at most 0.0043.
Values may be sent and summed in bfloat16 or wider, within the bound.
A program may use at most 64 MiB of HBM per device.

v0:
```python
import jax
import jax.numpy as jnp
from jax import lax
from jax.sharding import PartitionSpec as P

TEMP = 0.05
SHARP = 4.0


def shards(queries, gallery, positives, cutoffs):
    gathered = lax.all_gather(queries, "ga", axis=0, tiled=True)
    query_rows = gathered.shape[0]
    gallery_rows = gallery.shape[0]
    width = gallery.shape[1]
    positive_count = positives.shape[1]
    first_row = lax.axis_index("ga") * gallery_rows
    local_idx = positives - first_row
    owned_mask = (local_idx >= 0) & (local_idx < gallery_rows)
    clipped = jnp.clip(local_idx, 0, gallery_rows - 1)
    picked = gallery[clipped]
    direct = jnp.einsum("qpd,qd->qp", picked, gathered, preferred_element_type=jnp.float32)
    pos_scores = lax.psum(jnp.where(owned_mask, direct, 0.0), "ga")
    block_rows = min(512, query_rows)
    blocks = query_rows // block_rows

    def scores_of(index):
        rows_block = lax.dynamic_slice_in_dim(gathered, index * block_rows, block_rows, 0)
        return lax.dot_general(
            rows_block, gallery, (((1,), (1,)), ((), ())), preferred_element_type=jnp.float32
        )

    def rank_terms(index):
        scores = scores_of(index)
        anchor = lax.dynamic_slice_in_dim(pos_scores, index * block_rows, block_rows, 0)
        counted = []
        slopes = []
        for member in range(positive_count):
            squash = jax.nn.sigmoid((scores - anchor[:, member : member + 1]) / TEMP)
            counted.append(jnp.sum(squash, axis=1))
            slopes.append(jnp.sum(squash * (1.0 - squash), axis=1))
        return (jnp.stack(counted, axis=1), jnp.stack(slopes, axis=1), scores)

    block_ids = jnp.arange(blocks, dtype=jnp.int32)
    part_rank, part_slope, stored = lax.map(rank_terms, block_ids)
    part_rank = part_rank.reshape(query_rows, positive_count)
    part_slope = part_slope.reshape(query_rows, positive_count)
    rank_sum, slope_sum = lax.psum((part_rank, part_slope), "ga")
    rank_total = 0.5 + rank_sum
    slope_total = slope_sum / TEMP
    cut_values = cutoffs.astype(jnp.float32)
    recall = jax.nn.sigmoid(SHARP * (cut_values - rank_total[:, :, None]) / cut_values)
    weight_rank = jnp.sum(recall * (1.0 - recall) * SHARP / cut_values, axis=-1) / (
        positive_count * cut_values.shape[0]
    )
    own_spike = jnp.where(owned_mask, weight_rank * slope_total, 0.0)
    columns = lax.iota(jnp.int32, gallery_rows)

    def backward(gallery_acc, index):
        scores = stored[index]
        rows_block = lax.dynamic_slice_in_dim(gathered, index * block_rows, block_rows, 0)
        anchor = lax.dynamic_slice_in_dim(pos_scores, index * block_rows, block_rows, 0)
        coef_block = lax.dynamic_slice_in_dim(weight_rank, index * block_rows, block_rows, 0)
        spike_block = lax.dynamic_slice_in_dim(own_spike, index * block_rows, block_rows, 0)
        index_block = lax.dynamic_slice_in_dim(clipped, index * block_rows, block_rows, 0)
        weight = jnp.zeros(scores.shape, jnp.float32)
        for member in range(positive_count):
            squash = jax.nn.sigmoid((scores - anchor[:, member : member + 1]) / TEMP)
            weight = weight + coef_block[:, member : member + 1] * squash * (1.0 - squash) / TEMP
            hits = columns[None, :] == index_block[:, member : member + 1]
            weight = weight - jnp.where(hits, spike_block[:, member : member + 1], 0.0)
        dscore = weight.astype(jnp.bfloat16)
        query_part = jnp.dot(dscore, gallery, preferred_element_type=jnp.float32)
        gallery_acc = gallery_acc + lax.dot_general(
            dscore, rows_block, (((0,), (0,)), ((), ())), preferred_element_type=jnp.float32
        )
        return (gallery_acc, query_part)

    start_acc = jnp.zeros((gallery_rows, width), jnp.float32)
    gallery_terms, query_terms = lax.scan(backward, start_acc, block_ids)
    query_terms = query_terms.reshape(query_rows, width)
    query_grad = lax.psum_scatter(query_terms, "ga", scatter_dimension=0, tiled=True)
    gallery_grad = lax.psum_scatter(gallery_terms, "pb", scatter_dimension=0, tiled=True)
    return (query_grad, gallery_grad)


def solution(mesh):
    placed = (P(("pb", "ga"), None), P("ga", None), P("pb", None), P())
    return jax.shard_map(
        shards,
        mesh=mesh,
        in_specs=placed,
        out_specs=(P(("pb", "ga"), None), P(("ga", "pb"), None)),
        check_vma=False,
    )
```

profile of v0, /device:TPU:16, one launch (start us, length us, event | category | flops | bytes accessed | tf_op | source)
XLA Modules:
  0.0 427.4 jit_solution(11065862056063354688)
XLA Ops:
  10.4 33.6 %gather_fusion = bf16[8192,512]{1,0:T(8,128)(2,1)} fusion(bf16[1536,512]{1,0:T(8,128)(2,1)S(1)} %copy-done, s32[8192]{0:T(1024)S(1)} %broadcast_clamp_fusion), kind=kCustom, calls=%fused_computation | custom fusion | bytes 16809984 | tf_op jit(solution)/shard_map/gather | solution.py:20
  44.0 12.6 %reshape.22 = bf16[2048,4,512]{2,1,0:T(4,128)(2,1)} reshape(bf16[8192,512]{1,0:T(8,128)(2,1)} %gather_fusion) | data formatting | bytes 16777216 | tf_op jit(solution)/shard_map/gather | solution.py:20
  56.6 3.1 all-gather.2.cloned.1.call-done
  59.8 7.7 %fusion.34 = f32[2048,1,4]{2,1,0:T(1,128)S(1)} fusion(bf16[2048,4,512]{2,1,0:T(4,128)(2,1)} %reshape.22, bf16[2048,512,1]{1,0,2:T(8,128)(2,1)} %bitcast.185), kind=kOutput, calls=%fused_computation.61 | convolution fusion | flops 8388608 | bytes 10518528 | tf_op jit(solution)/shard_map/qpd,qd->qp/dot_general | solution.py:21
  68.0 29.8 %psum.21 = f32[2048,4]{0,1:T(4,128)S(1)} all-reduce(f32[2048,4]{0,1:T(4,128)S(1)} %get-tuple-element.239), channel_id=1, replica_groups=mesh['pb'=4,'ga'=8] {'ga'}, use_global_device_ids=true, to_apply=%region_0.1 | all-reduce | flops 8192 | bytes 65536 | tf_op jit(solution)/shard_map/psum | solution.py:22
  97.8 41.1 %while.28 = (s32[]{:T(128)}, f32[4,512,4]{1,2,0:T(4,128)S(1)}, f32[4,512,4]{1,2,0:T(4,128)S(1)}, f32[4,512,1536]{2,1,0:T(8,128)}, s32[4]{0:T(128)S(1)}, /*index=...) while((s32[]{:T(128)}, f32[4,512,4]{1,2,0:T(4,128)S(1)}, ...), condition=%wide.region_10.11_spmd, body=%wide.region_1.10_spmd.sunk | while | flops 833626112 | bytes 36774160 | solution.py:44
  99.2 5.0 %add_divide_fusion.5 = (f32[512,1536]{1,0:T(8,128)S(1)}, f32[512,1536]{1,0:T(8,128)S(1)}, f32[512,1536]{1,0:T(8,128)S(1)}, f32[512,1536]{1,0:T(8,128)S(1)}, f32[512,1536]{1,0:T(8,128)S(1)}) fusion(f32[512]{0:T(512)S(1)} %bitcast.210, f32[512]{0:T(512)S(1)} %bitcast.213, f32[512]{0:T(512)S(1)} %bitcast.211, f32[512]{0:T(512)S(1)} %bitcast.212, ...), kind=kOutput, calls=%fused_computation.14.clone.1 | convolution fusion | flops 821035008 | bytes 17833988 | tf_op jit(solution)/shard_map/while/body/eval_jaxpr/dot_general | solution.py:28
  109.4 5.0 %add_divide_fusion.5 = (f32[512,1536]{1,0:T(8,128)S(1)}, f32[512,1536]{1,0:T(8,128)S(1)}, f32[512,1536]{1,0:T(8,128)S(1)}, f32[512,1536]{1,0:T(8,128)S(1)}, f32[512,1536]{1,0:T(8,128)S(1)}) fusion(f32[512]{0:T(512)S(1)} %bitcast.210, f32[512]{0:T(512)S(1)} %bitcast.213, f32[512]{0:T(512)S(1)} %bitcast.211, f32[512]{0:T(512)S(1)} %bitcast.212, ...), kind=kOutput, calls=%fused_computation.14.clone.1 | convolution fusion | flops 821035008 | bytes 17833988 | tf_op jit(solution)/shard_map/while/body/eval_jaxpr/dot_general | solution.py:28
  119.7 5.0 %add_divide_fusion.5 = (f32[512,1536]{1,0:T(8,128)S(1)}, f32[512,1536]{1,0:T(8,128)S(1)}, f32[512,1536]{1,0:T(8,128)S(1)}, f32[512,1536]{1,0:T(8,128)S(1)}, f32[512,1536]{1,0:T(8,128)S(1)}) fusion(f32[512]{0:T(512)S(1)} %bitcast.210, f32[512]{0:T(512)S(1)} %bitcast.213, f32[512]{0:T(512)S(1)} %bitcast.211, f32[512]{0:T(512)S(1)} %bitcast.212, ...), kind=kOutput, calls=%fused_computation.14.clone.1 | convolution fusion | flops 821035008 | bytes 17833988 | tf_op jit(solution)/shard_map/while/body/eval_jaxpr/dot_general | solution.py:28
  130.0 5.0 %add_divide_fusion.5 = (f32[512,1536]{1,0:T(8,128)S(1)}, f32[512,1536]{1,0:T(8,128)S(1)}, f32[512,1536]{1,0:T(8,128)S(1)}, f32[512,1536]{1,0:T(8,128)S(1)}, f32[512,1536]{1,0:T(8,128)S(1)}) fusion(f32[512]{0:T(512)S(1)} %bitcast.210, f32[512]{0:T(512)S(1)} %bitcast.213, f32[512]{0:T(512)S(1)} %bitcast.211, f32[512]{0:T(512)S(1)} %bitcast.212, ...), kind=kOutput, calls=%fused_computation.14.clone.1 | convolution fusion | flops 821035008 | bytes 17833988 | tf_op jit(solution)/shard_map/while/body/eval_jaxpr/dot_general | solution.py:28
  139.6 71.5 %all-reduce.3.cloned.1.call-done = (f32[2048,4]{0,1:T(4,128)}, f32[2048,4]{0,1:T(4,128)}) async-done(((f32[2048,4]{0,1:T(4,128)}, f32[2048,4]{0,1:T(4,128)}), (f32[2048,4]{0,1:T(4,128)}, f32[2048,4]{0,1:T(4,128)})) %all-reduce.3.cloned.1.call-update) | async-done | bytes 65552 | tf_op jit(solution)/shard_map/psum | solution.py:47
  213.0 77.1 %while.29 = (s32[]{:T(128)}, f32[1536,512]{1,0:T(8,128)}, f32[4,512,512]{2,1,0:T(8,128)}, s32[4]{0:T(128)S(1)}, f32[2048,4]{0,1:T(4,128)S(1)}, /*index=5*/f32[4,...) while((s32[]{:T(128)}, f32[1536,512]{1,0:T(8,128)}, ...), condition=%wide.region_15.16_spmd.clone.clone, body=%wide.region_14.15_spmd.clone.clone.sunk | while | flops 1653080064 | bytes 17400188 | solution.py:79
  217.3 8.5 %subtract_convert_fusion.2 = bf16[512,1536]{1,0:T(8,128)(2,1)S(1)} fusion(f32[4,512,1536]{2,1,0:T(8,128)} %get-tuple-element.550, s32[]{:T(128)S(6)} %select_n.71, f32[512]{0:T(512)S(1)} %bitcast.197, s32[512]{0:T(512)S(1)} %bitcast.201, f32[512]{0:T(512)S(1)} %bitcast.205, f32[512]{0:T(512)S(1)} %bitcast.206, f32[512]{0:T(512)S(1)} %bitcast.195, ...), kind=kLoop, calls=%fused_computation.52.clone.1 | loop fusion | flops 40894464 | bytes 4751364 | tf_op jit(solution)/shard_map/while/body/eval_jaxpr/convert_element_type | solution.py:71
  225.8 3.7 convolution_add_fusion.2
  229.5 2.0 fusion.65
  235.8 8.5 %subtract_convert_fusion.2 = bf16[512,1536]{1,0:T(8,128)(2,1)S(1)} fusion(f32[4,512,1536]{2,1,0:T(8,128)} %get-tuple-element.550, s32[]{:T(128)S(6)} %select_n.71, f32[512]{0:T(512)S(1)} %bitcast.197, s32[512]{0:T(512)S(1)} %bitcast.201, f32[512]{0:T(512)S(1)} %bitcast.205, f32[512]{0:T(512)S(1)} %bitcast.206, f32[512]{0:T(512)S(1)} %bitcast.195, ...), kind=kLoop, calls=%fused_computation.52.clone.1 | loop fusion | flops 40894464 | bytes 4751364 | tf_op jit(solution)/shard_map/while/body/eval_jaxpr/convert_element_type | solution.py:71
  244.3 4.8 %convolution_add_fusion.2 = f32[1536,512]{1,0:T(8,128)} fusion(bf16[512,1536]{1,0:T(8,128)(2,1)S(1)} %subtract_convert_fusion.2, f32[1536,512]{1,0:T(8,128)} %get-tuple-element.527, pred[]{:T(512)S(6)} %compare.3, bf16[2048,512]{1,0:T(8,128)(2,1)} %get-tuple-element.554, s32[]{:T(128)S(6)} %select_n.72), kind=kOutput, calls=%fused_computation.27.clone.1 | convolution fusion | flops 806879232 | bytes 8388613 | tf_op jit(solution)/shard_map/while/body/eval_jaxpr/dot_general | solution.py:73
  255.4 8.5 %subtract_convert_fusion.2 = bf16[512,1536]{1,0:T(8,128)(2,1)S(1)} fusion(f32[4,512,1536]{2,1,0:T(8,128)} %get-tuple-element.550, s32[]{:T(128)S(6)} %select_n.71, f32[512]{0:T(512)S(1)} %bitcast.197, s32[512]{0:T(512)S(1)} %bitcast.201, f32[512]{0:T(512)S(1)} %bitcast.205, f32[512]{0:T(512)S(1)} %bitcast.206, f32[512]{0:T(512)S(1)} %bitcast.195, ...), kind=kLoop, calls=%fused_computation.52.clone.1 | loop fusion | flops 40894464 | bytes 4751364 | tf_op jit(solution)/shard_map/while/body/eval_jaxpr/convert_element_type | solution.py:71
  263.9 4.7 %convolution_add_fusion.2 = f32[1536,512]{1,0:T(8,128)} fusion(bf16[512,1536]{1,0:T(8,128)(2,1)S(1)} %subtract_convert_fusion.2, f32[1536,512]{1,0:T(8,128)} %get-tuple-element.527, pred[]{:T(512)S(6)} %compare.3, bf16[2048,512]{1,0:T(8,128)(2,1)} %get-tuple-element.554, s32[]{:T(128)S(6)} %select_n.72), kind=kOutput, calls=%fused_computation.27.clone.1 | convolution fusion | flops 806879232 | bytes 8388613 | tf_op jit(solution)/shard_map/while/body/eval_jaxpr/dot_general | solution.py:73
  274.9 8.5 %subtract_convert_fusion.2 = bf16[512,1536]{1,0:T(8,128)(2,1)S(1)} fusion(f32[4,512,1536]{2,1,0:T(8,128)} %get-tuple-element.550, s32[]{:T(128)S(6)} %select_n.71, f32[512]{0:T(512)S(1)} %bitcast.197, s32[512]{0:T(512)S(1)} %bitcast.201, f32[512]{0:T(512)S(1)} %bitcast.205, f32[512]{0:T(512)S(1)} %bitcast.206, f32[512]{0:T(512)S(1)} %bitcast.195, ...), kind=kLoop, calls=%fused_computation.52.clone.1 | loop fusion | flops 40894464 | bytes 4751364 | tf_op jit(solution)/shard_map/while/body/eval_jaxpr/convert_element_type | solution.py:71
  283.4 4.7 %convolution_add_fusion.2 = f32[1536,512]{1,0:T(8,128)} fusion(bf16[512,1536]{1,0:T(8,128)(2,1)S(1)} %subtract_convert_fusion.2, f32[1536,512]{1,0:T(8,128)} %get-tuple-element.527, pred[]{:T(512)S(6)} %compare.3, bf16[2048,512]{1,0:T(8,128)(2,1)} %get-tuple-element.554, s32[]{:T(128)S(6)} %select_n.72), kind=kOutput, calls=%fused_computation.27.clone.1 | convolution fusion | flops 806879232 | bytes 8388613 | tf_op jit(solution)/shard_map/while/body/eval_jaxpr/dot_general | solution.py:73
  288.1 2.0 fusion.65
  290.7 38.1 %reduce-scatter.5.cloned.1.call-done = f32[384,512]{1,0:T(8,128)} async-done(((f32[1536,512]{1,0:T(8,128)}), f32[384,512]{1,0:T(8,128)}) %reduce-scatter.5.cloned.1.call-update) | async-done | bytes 786448 | tf_op jit(solution)/shard_map/reduce_scatter | solution.py:82
  328.8 92.1 %reduce-scatter.3.cloned.1.call-done = f32[256,512]{1,0:T(8,128)} async-done(((f32[2048,512]{1,0:T(8,128)}), f32[256,512]{1,0:T(8,128)}) %reduce-scatter.3.cloned.1.call-update) | async-done | bytes 524304 | tf_op jit(solution)/shard_map/reduce_scatter | solution.py:81
  (85 shorter events, 36.3 us)
Async XLA Ops:
  7.2 3.2 copy-start
  7.2 52.6 %all-gather.2.cloned.1.call-start = ((), (), s32[]{:S(2)}) async-start(), calls=%async_computation.2 | async-start | bytes 2359296 | tf_op jit(solution)/shard_map/all_gather | solution.py:11
  7.9 203.2 %all-reduce.3.cloned.1.call-start = ((), (), s32[]{:S(2)}) async-start(), calls=%async_computation.5 | async-start | bytes 131072 | tf_op jit(solution)/shard_map/psum | solution.py:47
  59.7 8.2 %copy-start.1 = (s32[2048,4]{0,1:T(4,128)S(1)}, s32[2048,4]{0,1:T(4,128)}, u32[]{:S(2)}) copy-start(s32[2048,4]{0,1:T(4,128)} %param.10) | copy-start | bytes 98308
  97.8 41.8 %copy-start.4 = (s32[4]{0:T(128)S(1)}, s32[4]{0:T(128)}, u32[]{:S(2)}) copy-start(s32[4]{0:T(128)} %param.11) | copy-start | bytes 52
  138.9 0.6 copy-start.2
  138.9 0.6 copy-start.3
  139.6 189.2 %reduce-scatter.5.cloned.1.call-start = ((), (), s32[]{:S(2)}) async-start(), calls=%async_computation.4 | async-start | bytes 3932160 | tf_op jit(solution)/shard_map/reduce_scatter | solution.py:82
  290.1 130.7 %reduce-scatter.3.cloned.1.call-start = ((), (), s32[]{:S(2)}) async-start(), calls=%async_computation.3 | async-start | bytes 4718592 | tf_op jit(solution)/shard_map/reduce_scatter | solution.py:81
Sparse Core Ops, SparseCore 0:
  10.1 49.5 all-gather.1
  139.7 71.4 all-reduce.2
  290.2 38.5 reduce-scatter.4
  332.9 87.9 reduce-scatter.2
where the time goes:
time: 431 us; the launch traced here: 427 us
  waiting for transfers between devices  206 us (48%)
  local copies, waits for them, and re-layouts  65.5 us (15%)
  matrix products  53.4 us (12%)
  other arithmetic  45.6 us (11%)
  blocking collectives  29.8 us (7%)
  between operations  13.9 us (3%)
  loops' own time  13 us (3%)
    reduce_scatter x1, waiting for transfers between devices, shards(): lax.psum_scatter(query_terms, 'ga', scatter_dimension=0, tiled=True)  92.1 us
    psum x1, waiting for transfers between devices, shards(): rank_sum, slope_sum = lax.psum((part_rank, part_slope), 'ga')  71.5 us
    gather x2, local copies, waits for them, and re-layouts, shards(): picked = gallery[clipped]  46.2 us
    reduce_scatter x1, waiting for transfers between devices, shards(): lax.psum_scatter(gallery_terms, 'pb', scatter_dimension=0, tiled=True)  38.1 us
    convert_element_type x4, other arithmetic, backward(): dscore = weight.astype(jnp.bfloat16)  34 us
    psum x1, blocking collectives, shards(): pos_scores = lax.psum(jnp.where(owned_mask, direct, 0.0), 'ga')  29.8 us
    dot_general x4, matrix products, scores_of(): lax.dot_general(rows_block, gallery, (((1,), (1,)), ((), ())), preferred_...  19.8 us
    dot_general x4, matrix products, backward(): lax.dot_general(dscore, rows_block, (((0,), (0,)), ((), ())), preferred_e...  18 us
  transfers between devices with their start and end apart: 4, of which 4 were waited for; matrix products, arithmetic and copies ran while one was open for 11% of the time, Pallas kernels for 0%

commit v1 on v0

v1 whole, which is shorter than its diff:
```python
import functools

import jax
import jax.numpy as jnp
from jax import lax
from jax.experimental import pallas as pl
from jax.experimental.pallas import tpu as pltpu
from jax.sharding import PartitionSpec as P

TEMP = 0.05
SHARP = 4.0
LANES = 128
GROUP = 16
MESH = pl.DeviceIdType.MESH


def kernel(
    n, npb, cut_ref, q_ref, g_ref, idx_ref, qout_ref, gout_ref,
    qs, sc, dsc, pos_in, rank_in, stage, cols, qp_out, qp_in,
    gal_f, gal_b, ga_in, gb_out, gb_in,
    q_send, q_recv, pos_send, pos_recv, rank_send, rank_recv, qp_send, qp_recv,
    ga_send, ga_recv, gb_send, gb_recv,
):
    rows, width = q_ref.shape
    gal = g_ref.shape[0]
    members = idx_ref.shape[1]
    cuts = cut_ref.shape[0]
    chunks = gal // LANES
    nx = npb // 2
    cols_x = gal // nx
    half = cols_x // 2
    per_x = cols_x // LANES
    me = lax.axis_index("ga")
    mp = lax.axis_index("pb")
    my_x = mp // 2
    core = lax.rem(mp, 2)
    partner = mp + 1 - 2 * core
    groups = rows // GROUP

    barrier = pltpu.get_barrier_semaphore()
    for p in range(1, n):
        pl.semaphore_signal(barrier, inc=1, device_id={"ga": lax.rem(me + p, n)}, device_id_type=MESH)
    for p in range(1, npb):
        pl.semaphore_signal(barrier, inc=1, device_id={"pb": lax.rem(mp + p, npb)}, device_id_type=MESH)
    pl.semaphore_wait(barrier, n - 1 + npb - 1)

    def query_copy(p):
        return pltpu.make_async_remote_copy(
            src_ref=q_ref, dst_ref=qs.at[p], send_sem=q_send.at[p], recv_sem=q_recv.at[p],
            device_id={"ga": lax.rem(me + p, n)}, device_id_type=MESH)

    for p in range(1, n):
        query_copy(p).start()
    qs[0] = q_ref[...]

    lane = lax.broadcasted_iota(jnp.int32, (GROUP, LANES), 1)

    def spread(column):
        return jnp.broadcast_to(column, (GROUP, LANES))

    def keys_of(r, i):
        owner = lax.rem(me - r + n, n)
        start = pl.multiple_of(owner * rows + i * GROUP, GROUP)
        local = idx_ref[pl.ds(start, GROUP), :] - me * gal
        return [spread(local[:, m:m + 1]) - lane for m in range(members)]

    def exchange(buf, r, send, recv):
        @pl.loop(1, n)
        def _(p):
            pltpu.make_async_remote_copy(
                src_ref=buf.at[r, 0], dst_ref=buf.at[lax.rem(r + p, n), p],
                send_sem=send.at[r], recv_sem=recv.at[lax.rem(r + p, n)],
                device_id={"ga": lax.rem(me + p, n)}, device_id_type=MESH).start()

    def exchange_wait(buf, r, send, recv):
        return pltpu.make_async_remote_copy(
            src_ref=buf.at[r, pl.ds(1, n - 1)], dst_ref=buf.at[r, pl.ds(1, n - 1)],
            send_sem=send.at[r], recv_sem=recv.at[r],
            device_id={"ga": lax.rem(me + 1, n)}, device_id_type=MESH)

    def to_lanes(values):
        out = jnp.zeros((GROUP, LANES), jnp.float32)
        for k, value in enumerate(values):
            out = jnp.where(lane == k, spread(value), out)
        return out

    @pl.loop(0, n)
    def _(r):
        @pl.when(r > 0)
        def _():
            query_copy(r).wait_recv()

        sc[r] = lax.dot_general(
            qs[r], g_ref[...], (((1,), (1,)), ((), ())), preferred_element_type=jnp.float32)

        @pl.loop(0, groups)
        def _(i):
            at = pl.ds(pl.multiple_of(i * GROUP, GROUP), GROUP)
            keys = keys_of(r, i)
            picked = [jnp.zeros((GROUP, LANES), jnp.float32) for _ in range(members)]
            for c in range(chunks):
                s = sc[r, at, c * LANES:(c + 1) * LANES] * (0.5 / TEMP)
                sc[r, at, c * LANES:(c + 1) * LANES] = s
                picked = [jnp.where(keys[m] == c * LANES, s, picked[m]) for m in range(members)]
            stage[at, :] = to_lanes([jnp.sum(x, axis=1, keepdims=True) for x in picked])

        pos_in[r, 0] = jnp.transpose(stage[...])[:8]
        exchange(pos_in, r, pos_send, pos_recv)

    @pl.loop(0, n)
    def _(r):
        exchange_wait(pos_in, r, pos_send, pos_recv).wait_recv()
        anchor = jnp.sum(pos_in[r], axis=0)
        cols[r, 0] = jnp.transpose(anchor)

        @pl.loop(0, groups)
        def _(i):
            at = pl.ds(pl.multiple_of(i * GROUP, GROUP), GROUP)
            anchors = cols[r, 0, at, :]
            a = [spread(anchors[:, m:m + 1]) for m in range(members)]
            total = [jnp.zeros((GROUP, LANES), jnp.float32) for _ in range(members)]
            square = [jnp.zeros((GROUP, LANES), jnp.float32) for _ in range(members)]
            for c in range(chunks):
                s = sc[r, at, c * LANES:(c + 1) * LANES]
                for m in range(members):
                    u = 1.0 + jnp.tanh(s - a[m])
                    total[m] = total[m] + u
                    square[m] = square[m] + u * u
            sums = [jnp.sum(x, axis=1, keepdims=True) for x in total]
            slopes = [
                jnp.sum(2.0 * x - y, axis=1, keepdims=True) for x, y in zip(total, square)]
            stage[at, :] = to_lanes(sums + slopes)

        rank_in[r, 0] = jnp.transpose(stage[...])[:2 * members]
        exchange(rank_in, r, rank_send, rank_recv)

    @pl.loop(0, n)
    def _(r):
        exchange_wait(rank_in, r, rank_send, rank_recv).wait_recv()
        both = jnp.sum(rank_in[r], axis=0)
        rank = 0.5 + 0.5 * both[:members]
        slope = both[members:] * (0.25 / TEMP)
        wr = jnp.zeros(rank.shape, jnp.float32)
        for c in range(cuts):
            kv = jnp.full(rank.shape, cut_ref[c], jnp.int32).astype(jnp.float32)
            e = jnp.exp(-jnp.abs(SHARP * (kv - rank) / kv))
            wr = wr + e / ((1.0 + e) * (1.0 + e)) * SHARP / kv
        wr = wr / (members * cuts)
        cols[r, 1] = jnp.transpose(jnp.concatenate([wr * (0.25 / TEMP), wr * slope], axis=0))

        @pl.loop(0, groups)
        def _(i):
            at = pl.ds(pl.multiple_of(i * GROUP, GROUP), GROUP)
            at_all = pl.ds(pl.multiple_of(r * rows + i * GROUP, GROUP), GROUP)
            keys = keys_of(r, i)
            anchors = cols[r, 0, at, :]
            weights = cols[r, 1, at, :]
            a = [spread(anchors[:, m:m + 1]) for m in range(members)]
            w = [spread(weights[:, m:m + 1]) for m in range(members)]
            spike = [spread(weights[:, members + m:members + m + 1]) for m in range(members)]
            base = sum(w[1:], w[0])
            for c in range(chunks):
                s = sc[r, at, c * LANES:(c + 1) * LANES]
                d = base
                for m in range(members):
                    t = jnp.tanh(s - a[m])
                    d = d - w[m] * (t * t)
                for m in range(members):
                    d = d - jnp.where(keys[m] == c * LANES, spike[m], 0.0)
                k = c % per_x
                dsc[c // per_x, at_all, k * LANES:(k + 1) * LANES] = d.astype(jnp.bfloat16)

        part = jnp.zeros((rows, width), jnp.float32)
        block = pl.ds(pl.multiple_of(r * rows, rows), rows)
        for x in range(nx):
            part = part + jnp.dot(
                dsc[x, block, :], g_ref[x * cols_x:(x + 1) * cols_x, :],
                preferred_element_type=jnp.float32)

        @pl.when(r == 0)
        def _():
            qout_ref[...] = part

        @pl.when(r > 0)
        def _():
            qp_out[r] = part.astype(jnp.bfloat16)
            pltpu.make_async_remote_copy(
                src_ref=qp_out.at[r], dst_ref=qp_in.at[r], send_sem=qp_send.at[r], recv_sem=qp_recv.at[r],
                device_id={"ga": lax.rem(me - r + n, n)}, device_id_type=MESH).start()

    def pair_copy(x):
        return pltpu.make_async_remote_copy(
            src_ref=gal_b.at[x, 1 - core], dst_ref=ga_in.at[x], send_sem=ga_send.at[x], recv_sem=ga_recv.at[x],
            device_id={"pb": partner}, device_id_type=MESH)

    def chip_copy(k):
        return pltpu.make_async_remote_copy(
            src_ref=gb_out.at[k], dst_ref=gb_in.at[k], send_sem=gb_send.at[k], recv_sem=gb_recv.at[k],
            device_id={"pb": lax.rem(my_x + 1 + k, nx) * 2 + core}, device_id_type=MESH)

    qall = qs[...].reshape(n * rows, width)
    for k in range(nx):
        x = lax.rem(my_x + 1 + k, nx)
        for h in range(2):
            res = lax.dot_general(
                dsc[x, :, h * half:(h + 1) * half], qall, (((0,), (0,)), ((), ())),
                preferred_element_type=jnp.float32)
            gal_f[x, h] = res
            gal_b[x, h] = res.astype(jnp.bfloat16)
        pair_copy(x).start()

    for k in range(nx - 1):
        x = lax.rem(my_x + 1 + k, nx)
        pair_copy(x).wait_recv()
        gb_out[k] = (gal_f[x, core] + ga_in[x].astype(jnp.float32)).astype(jnp.bfloat16)
        chip_copy(k).start()
    pair_copy(my_x).wait_recv()
    gout_ref[...] = gal_f[my_x, core] + ga_in[my_x].astype(jnp.float32)

    @pl.loop(1, n)
    def _(r):
        pltpu.make_async_remote_copy(
            src_ref=qp_out.at[r], dst_ref=qp_in.at[r], send_sem=qp_send.at[r], recv_sem=qp_recv.at[r],
            device_id={"ga": lax.rem(me - r + n, n)}, device_id_type=MESH).wait()
        qout_ref[...] += qp_in[r].astype(jnp.float32)
        query_copy(r).wait_send()

    for k in range(nx - 1):
        chip_copy(k).wait()
        gout_ref[...] += gb_in[k].astype(jnp.float32)

    @pl.loop(0, n)
    def _(r):
        exchange_wait(pos_in, r, pos_send, pos_recv).wait_send()
        exchange_wait(rank_in, r, rank_send, rank_recv).wait_send()

    @pl.loop(0, nx)
    def _(x):
        pair_copy(x).wait_send()


def shards(n, npb, queries, gallery, positives, cutoffs):
    rows, width = queries.shape
    gal = gallery.shape[0]
    members = positives.shape[1]
    nx = npb // 2
    half = gal // npb
    dma = pltpu.SemaphoreType.DMA
    vmem = pl.BlockSpec(memory_space=pltpu.VMEM)
    f32, bf16 = jnp.float32, jnp.bfloat16
    return pl.pallas_call(
        functools.partial(kernel, n, npb),
        out_shape=(
            jax.ShapeDtypeStruct((rows, width), f32),
            jax.ShapeDtypeStruct((half, width), f32),
        ),
        in_specs=[pl.BlockSpec(memory_space=pltpu.SMEM), vmem, vmem, vmem],
        out_specs=(vmem, vmem),
        scratch_shapes=[
            pltpu.VMEM((n, rows, width), bf16),
            pltpu.VMEM((n, rows, gal), f32),
            pltpu.VMEM((nx, n * rows, gal // nx), bf16),
            pltpu.VMEM((n, n, 8, rows), f32),
            pltpu.VMEM((n, n, 2 * members, rows), f32),
            pltpu.VMEM((rows, LANES), f32),
            pltpu.VMEM((n, 2, rows, 8), f32),
            pltpu.VMEM((n, rows, width), bf16),
            pltpu.VMEM((n, rows, width), bf16),
            pltpu.VMEM((nx, 2, half, width), f32),
            pltpu.VMEM((nx, 2, half, width), bf16),
            pltpu.VMEM((nx, half, width), bf16),
            pltpu.VMEM((max(nx - 1, 1), half, width), bf16),
            pltpu.VMEM((max(nx - 1, 1), half, width), bf16),
            dma((n,)), dma((n,)), dma((n,)), dma((n,)), dma((n,)), dma((n,)), dma((n,)), dma((n,)),
            dma((nx,)), dma((nx,)), dma((nx,)), dma((nx,)),
        ],
        compiler_params=pltpu.CompilerParams(
            collective_id=0, has_side_effects=True, vmem_limit_bytes=62 * 1024 * 1024),
    )(cutoffs, queries, gallery, positives)


def solution(mesh):
    placed = (P(("pb", "ga"), None), P("ga", None), P("pb", None), P())
    return jax.shard_map(
        functools.partial(shards, mesh.shape["ga"], mesh.shape["pb"]),
        mesh=mesh,
        in_specs=placed,
        out_specs=(P(("pb", "ga"), None), P(("ga", "pb"), None)),
        check_vma=False,
    )
```

time: 431 us -> 175 us (0.41)
  waiting for transfers between devices: 206 us -> 0 us
  Pallas kernels: 0 us -> 169 us
  local copies, waits for them, and re-layouts: 65.5 us -> 4.93 us
  matrix products: 53.4 us -> 0 us
  other arithmetic: 45.6 us -> 0 us
  blocking collectives: 29.8 us -> 0 us
  between operations: 13.9 us -> 0.65 us
  loops' own time: 13 us -> 0 us
    pallas_call x0 -> x1, Pallas kernels: none -> 169 us  [shards(): pl.pallas_call(functools.partial(kernel, n, npb), out_shape=(jax.ShapeDty...]
    reduce_scatter x2 -> x0, waiting for transfers between devices: 130 us -> none  [the longest x1 92.1 us: shards(): lax.psum_scatter(query_terms, 'ga', scatter_dimension=0, tiled=True)]
    psum x1 -> x0, waiting for transfers between devices: 71.5 us -> none  [shards(): rank_sum, slope_sum = lax.psum((part_rank, part_slope), 'ga')]
    dot_general x13 -> x0, matrix products: 53.4 us -> none  [the longest x4 19.8 us: scores_of(): lax.dot_general(rows_block, gallery, (((1,), (1,)), ((), ())), preferred_...]
    gather x2 -> x0, local copies, waits for them, and re-layouts: 46.2 us -> none  [shards(): picked = gallery[clipped]]
    convert_element_type x5 -> x0, other arithmetic: 34 us -> none  [the longest x4 34 us: backward(): dscore = weight.astype(jnp.bfloat16)]
    psum x1 -> x0, blocking collectives: 29.8 us -> none  [shards(): pos_scores = lax.psum(jnp.where(owned_mask, direct, 0.0), 'ga')]
    another operation x2 -> x0, loops' own time: 13 us -> none  [the longest x1 10.5 us: shards(): gallery_terms, query_terms = lax.scan(backward, start_acc, block_ids)]
  transfers between devices with their start and end apart: 4 -> 0, of which waited for: 4 -> 0; matrix products, arithmetic and copies ran while one was open for 11% -> 0% of each run, Pallas kernels for 0% -> 0%
where the time goes in v1:
time: 175 us; the launch traced here: 174 us
  Pallas kernels  169 us (97%)
  local copies, waits for them, and re-layouts  4.93 us (3%)
    pallas_call x1, Pallas kernels, shards(): pl.pallas_call(functools.partial(kernel, n, npb), out_shape=(jax.ShapeDty...  169 us
    unnamed x5, local copies, waits for them, and re-layouts  4.93 us

profile of v1, /device:TPU:16, one launch (start us, length us, event | category | flops | bytes accessed | tf_op | source)
XLA Modules:
  0.0 174.3 jit_solution(14793974177613320821)
XLA Ops:
  0.6 2.1 %copy.6.idx_ref = s32[2048,4]{1,0:T(8,128)} copy(s32[2048,4]{0,1:T(4,128)} %param.6) | data formatting | bytes 65536 | tf_op args[2]
  2.7 168.8 %shard_map.59 = (f32[256,512]{1,0:T(8,128)}, f32[384,512]{1,0:T(8,128)}) custom-call(s32[4]{0:T(128)} %cut_ref.1, bf16[256,512]{1,0:T(8,128)(2,1)} %q_ref.1, bf16[1536,512]{1,0:T(8,128)(2,1)} %g_ref.1, s32[2048,4]{1,0:T(8,128)} %copy.6.idx_ref), custom_call_target="tpu_custom_call" | custom-call | tf_op jit(solution)/shard_map/pallas_call | solution.py:251
  171.5 0.0 copy-start
  171.5 1.9 %copy.9 = f32[256,512]{1,0:T(8,128)} copy(f32[256,512]{1,0:T(8,128)} %get-tuple-element.4) | data formatting | bytes 1048576
  173.5 0.0 copy-done
  173.5 0.9 copy.10
Async XLA Ops:
  171.5 2.0 %copy-start = (f32[384,512]{1,0:T(8,128)S(1)}, f32[384,512]{1,0:T(8,128)}, u32[]{:S(2)}) copy-start(f32[384,512]{1,0:T(8,128)} %get-tuple-element.5) | copy-start | bytes 2359300

commit v2 on v1

--- a/solution.py
+++ b/solution.py
@@ -17,8 +17,8 @@
 def kernel(
     n, npb, cut_ref, q_ref, g_ref, idx_ref, qout_ref, gout_ref,
     qs, sc, dsc, pos_in, rank_in, stage, cols, qp_out, qp_in,
-    gal_f, gal_b, ga_in, gb_out, gb_in,
-    q_send, q_recv, pos_send, pos_recv, rank_send, rank_recv, qp_send, qp_recv,
+    own_part, z_out, z_in, gal_f, gal_b, ga_in, gb_out, gb_in,
+    q_send, q_recv, pos_send, pos_recv, rank_send, rank_recv, y_send, y_recv, z_send, z_recv,
     ga_send, ga_recv, gb_send, gb_recv,
 ):
     rows, width = q_ref.shape
@@ -36,6 +36,11 @@
     core = lax.rem(mp, 2)
     partner = mp + 1 - 2 * core
     groups = rows // GROUP
+    depth = n // 2
+    z = me // 2
+    y = lax.rem(me, 2)
+    across = z * 2 + 1 - y
+    hr = rows // 2
 
     barrier = pltpu.get_barrier_semaphore()
     for p in range(1, n):
@@ -44,22 +49,45 @@
         pl.semaphore_signal(barrier, inc=1, device_id={"pb": lax.rem(mp + p, npb)}, device_id_type=MESH)
     pl.semaphore_wait(barrier, n - 1 + npb - 1)
 
-    def query_copy(p):
-        return pltpu.make_async_remote_copy(
-            src_ref=q_ref, dst_ref=qs.at[p], send_sem=q_send.at[p], recv_sem=q_recv.at[p],
-            device_id={"ga": lax.rem(me + p, n)}, device_id_type=MESH)
-
-    for p in range(1, n):
-        query_copy(p).start()
-    qs[0] = q_ref[...]
+    def hop(source, o, h, d, target):
+        return pltpu.make_async_remote_copy(
+            src_ref=source, dst_ref=qs.at[o, pl.ds(h * hr, hr)], send_sem=q_send.at[o, h, d],
+            recv_sem=q_recv.at[o, h], device_id={"ga": target}, device_id_type=MESH)
+
+    def hops(zo, yo, h, act, own=False):
+        o = zo * 2 + yo
+        source = q_ref.at[pl.ds(h * hr, hr)] if own else qs.at[o, pl.ds(h * hr, hr)]
+        along = (h == 1) | (yo == y)
+
+        @pl.when(along & (zo <= z) & (z < depth - 1))
+        def _():
+            act(hop(source, o, h, 0, lax.rem(me + 2, n)))
+
+        @pl.when(along & (zo >= z) & (z > 0))
+        def _():
+            act(hop(source, o, h, 1, lax.rem(me - 2 + n, n)))
+
+        @pl.when((yo == y) & ((h == 0) | (zo == z)))
+        def _():
+            act(hop(source, o, h, 2, across))
+
+    def candidate(j):
+        k = j // 2
+        step = (k + 1) // 2
+        zo = jnp.where(lax.rem(k, 2) == 1, z - step, z + step)
+        yo = jnp.where(lax.rem(j, 2) == 0, y, 1 - y)
+        return zo, yo, (zo >= 0) & (zo < depth)
+
+    for h in range(2):
+        hops(z, y, h, lambda c: c.start(), own=True)
+    qs[me] = q_ref[...]
 
     lane = lax.broadcasted_iota(jnp.int32, (GROUP, LANES), 1)
 
     def spread(column):
         return jnp.broadcast_to(column, (GROUP, LANES))
 
-    def keys_of(r, i):
-        owner = lax.rem(me - r + n, n)
+    def keys_of(owner, i):
         start = pl.multiple_of(owner * rows + i * GROUP, GROUP)
         local = idx_ref[pl.ds(start, GROUP), :] - me * gal
         return [spread(local[:, m:m + 1]) - lane for m in range(members)]
@@ -68,8 +96,8 @@
         @pl.loop(1, n)
         def _(p):
             pltpu.make_async_remote_copy(
-                src_ref=buf.at[r, 0], dst_ref=buf.at[lax.rem(r + p, n), p],
-                send_sem=send.at[r], recv_sem=recv.at[lax.rem(r + p, n)],
+                src_ref=buf.at[r, 0], dst_ref=buf.at[r, p],
+                send_sem=send.at[r], recv_sem=recv.at[r],
                 device_id={"ga": lax.rem(me + p, n)}, device_id_type=MESH).start()
 
     def exchange_wait(buf, r, send, recv):
@@ -84,12 +112,7 @@
             out = jnp.where(lane == k, spread(value), out)
         return out
 
-    @pl.loop(0, n)
-    def _(r):
-        @pl.when(r > 0)
-        def _():
-            query_copy(r).wait_recv()
-
+    def score_block(r):
         sc[r] = lax.dot_general(
             qs[r], g_ref[...], (((1,), (1,)), ((), ())), preferred_element_type=jnp.float32)
 
@@ -104,14 +127,28 @@
                 picked = [jnp.where(keys[m] == c * LANES, s, picked[m]) for m in range(members)]
             stage[at, :] = to_lanes([jnp.sum(x, axis=1, keepdims=True) for x in picked])
 
-        pos_in[r, 0] = jnp.transpose(stage[...])[:8]
+        pos_in[r, 0] = jnp.transpose(stage[...])[:members]
         exchange(pos_in, r, pos_send, pos_recv)
+
+    @pl.loop(0, 2 * (2 * depth - 1))
+    def _(j):
+        zo, yo, valid = candidate(j)
+
+        @pl.when(valid)
+        def _():
+            @pl.when(j > 0)
+            def _():
+                for h in range(2):
+                    hop(qs.at[zo * 2 + yo, pl.ds(h * hr, hr)], zo * 2 + yo, h, 0, across).wait_recv()
+                    hops(zo, yo, h, lambda c: c.start())
+
+            score_block(zo * 2 + yo)
 
     @pl.loop(0, n)
     def _(r):
         exchange_wait(pos_in, r, pos_send, pos_recv).wait_recv()
         anchor = jnp.sum(pos_in[r], axis=0)
-        cols[r, 0] = jnp.transpose(anchor)
+        cols[r, 0] = jnp.transpose(jnp.concatenate([anchor, anchor], axis=0))
 
         @pl.loop(0, groups)
         def _(i):
@@ -134,8 +171,22 @@
         rank_in[r, 0] = jnp.transpose(stage[...])[:2 * members]
         exchange(rank_in, r, rank_send, rank_recv)
 
+    def fold_copy(zo):
+        return pltpu.make_async_remote_copy(
+            src_ref=qp_out.at[zo], dst_ref=qp_in.at[zo], send_sem=y_send.at[zo], recv_sem=y_recv.at[zo],
+            device_id={"ga": across}, device_id_type=MESH)
+
+    def home_copy(k):
+        return pltpu.make_async_remote_copy(
+            src_ref=z_out.at[k], dst_ref=z_in.at[k], send_sem=z_send.at[k], recv_sem=z_recv.at[k],
+            device_id={"ga": lax.rem(z + k, depth) * 2 + y}, device_id_type=MESH)
+
     @pl.loop(0, n)
-    def _(r):
+    def _(t):
+        step = t // 2
+        first = lax.rem(t, 2) == 0
+        zo = lax.rem(z + 1 + step, depth)
+        r = zo * 2 + jnp.where(first, 1 - y, y)
         exchange_wait(rank_in, r, rank_send, rank_recv).wait_recv()
         both = jnp.sum(rank_in[r], axis=0)
         rank = 0.5 + 0.5 * both[:members]
@@ -177,16 +228,21 @@
                 dsc[x, block, :], g_ref[x * cols_x:(x + 1) * cols_x, :],
                 preferred_element_type=jnp.float32)
 
-        @pl.when(r == 0)
-        def _():
-            qout_ref[...] = part
-
-        @pl.when(r > 0)
-        def _():
-            qp_out[r] = part.astype(jnp.bfloat16)
-            pltpu.make_async_remote_copy(
-                src_ref=qp_out.at[r], dst_ref=qp_in.at[r], send_sem=qp_send.at[r], recv_sem=qp_recv.at[r],
-                device_id={"ga": lax.rem(me - r + n, n)}, device_id_type=MESH).start()
+        @pl.when(first)
+        def _():
+            qp_out[zo] = part.astype(jnp.bfloat16)
+            fold_copy(zo).start()
+
+        @pl.when(jnp.logical_not(first))
+        def _():
+            own_part[zo] = part
+
+            @pl.when(step > 0)
+            def _():
+                zf = lax.rem(z + step, depth)
+                fold_copy(zf).wait_recv()
+                z_out[step] = (own_part[zf] + qp_in[zf].astype(jnp.float32)).astype(jnp.bfloat16)
+                home_copy(step).start()
 
     def pair_copy(x):
         return pltpu.make_async_remote_copy(
@@ -217,13 +273,26 @@
     pair_copy(my_x).wait_recv()
     gout_ref[...] = gal_f[my_x, core] + ga_in[my_x].astype(jnp.float32)
 
-    @pl.loop(1, n)
-    def _(r):
-        pltpu.make_async_remote_copy(
-            src_ref=qp_out.at[r], dst_ref=qp_in.at[r], send_sem=qp_send.at[r], recv_sem=qp_recv.at[r],
-            device_id={"ga": lax.rem(me - r + n, n)}, device_id_type=MESH).wait()
-        qout_ref[...] += qp_in[r].astype(jnp.float32)
-        query_copy(r).wait_send()
+    fold_copy(z).wait_recv()
+    qout_ref[...] = own_part[z] + qp_in[z].astype(jnp.float32)
+
+    @pl.loop(1, depth)
+    def _(k):
+        home_copy(k).wait()
+        qout_ref[...] += z_in[k].astype(jnp.float32)
+
+    @pl.loop(0, depth)
+    def _(k):
+        fold_copy(k).wait_send()
+
+    @pl.loop(0, 2 * (2 * depth - 1))
+    def _(j):
+        zo, yo, valid = candidate(j)
+
+        @pl.when(valid)
+        def _():
+            for h in range(2):
+                hops(zo, yo, h, lambda c: c.wait_send())
 
     for k in range(nx - 1):
         chip_copy(k).wait()
@@ -260,18 +329,22 @@
             pltpu.VMEM((n, rows, width), bf16),
             pltpu.VMEM((n, rows, gal), f32),
             pltpu.VMEM((nx, n * rows, gal // nx), bf16),
-            pltpu.VMEM((n, n, 8, rows), f32),
+            pltpu.VMEM((n, n, members, rows), f32),
             pltpu.VMEM((n, n, 2 * members, rows), f32),
             pltpu.VMEM((rows, LANES), f32),
             pltpu.VMEM((n, 2, rows, 8), f32),
-            pltpu.VMEM((n, rows, width), bf16),
-            pltpu.VMEM((n, rows, width), bf16),
+            pltpu.VMEM((n // 2, rows, width), bf16),
+            pltpu.VMEM((n // 2, rows, width), bf16),
+            pltpu.VMEM((n // 2, rows, width), f32),
+            pltpu.VMEM((n // 2, rows, width), bf16),
+            pltpu.VMEM((n // 2, rows, width), bf16),
             pltpu.VMEM((nx, 2, half, width), f32),
             pltpu.VMEM((nx, 2, half, width), bf16),
             pltpu.VMEM((nx, half, width), bf16),
             pltpu.VMEM((max(nx - 1, 1), half, width), bf16),
             pltpu.VMEM((max(nx - 1, 1), half, width), bf16),
-            dma((n,)), dma((n,)), dma((n,)), dma((n,)), dma((n,)), dma((n,)), dma((n,)), dma((n,)),
+            dma((n, 2, 3)), dma((n, 2)), dma((n,)), dma((n,)), dma((n,)), dma((n,)),
+            dma((n // 2,)), dma((n // 2,)), dma((n // 2,)), dma((n // 2,)),
             dma((nx,)), dma((nx,)), dma((nx,)), dma((nx,)),
         ],
         compiler_params=pltpu.CompilerParams(

time: 175 us -> 139 us (0.79)
  Pallas kernels: 169 us -> 133 us
    pallas_call x1, Pallas kernels: 169 us -> 133 us  [shards(): pl.pallas_call(functools.partial(kernel, n, npb), out_shape=(jax.ShapeDty...]
where the time goes in v2:
time: 139 us
  Pallas kernels  133 us (96%)
  local copies, waits for them, and re-layouts  4.93 us (4%)
    pallas_call x1, Pallas kernels, shards(): pl.pallas_call(functools.partial(kernel, n, npb), out_shape=(jax.ShapeDty...  133 us
    unnamed x5, local copies, waits for them, and re-layouts  4.93 us

profile of v2, /device:TPU:16, one launch (start us, length us, event | category | flops | bytes accessed | tf_op | source)
XLA Modules:
  0.0 138.8 jit_solution(6693410240410184153)
XLA Ops:
  0.6 2.1 %copy.6.idx_ref = s32[2048,4]{1,0:T(8,128)} copy(s32[2048,4]{0,1:T(4,128)} %param.6) | data formatting | bytes 65536 | tf_op args[2]
  2.7 133.2 %shard_map.59 = (f32[256,512]{1,0:T(8,128)}, f32[384,512]{1,0:T(8,128)}) custom-call(s32[4]{0:T(128)} %cut_ref.1, bf16[256,512]{1,0:T(8,128)(2,1)} %q_ref.1, bf16[1536,512]{1,0:T(8,128)(2,1)} %g_ref.1, s32[2048,4]{1,0:T(8,128)} %copy.6.idx_ref), custom_call_target="tpu_custom_call" | custom-call | tf_op jit(solution)/shard_map/pallas_call | solution.py:320
  135.9 0.0 copy-start
  135.9 1.9 %copy.9 = f32[256,512]{1,0:T(8,128)} copy(f32[256,512]{1,0:T(8,128)} %get-tuple-element.4) | data formatting | bytes 1048576
  137.9 0.0 copy-done
  137.9 0.9 copy.10
Async XLA Ops:
  135.9 2.0 %copy-start = (f32[384,512]{1,0:T(8,128)S(1)}, f32[384,512]{1,0:T(8,128)}, u32[]{:S(2)}) copy-start(f32[384,512]{1,0:T(8,128)} %get-tuple-element.5) | copy-start | bytes 2359300

commit v3 on v2

--- a/solution.py
+++ b/solution.py
@@ -10,7 +10,7 @@
 TEMP = 0.05
 SHARP = 4.0
 LANES = 128
-GROUP = 16
+GROUP = 32
 MESH = pl.DeviceIdType.MESH
 
 
@@ -116,7 +116,7 @@
         sc[r] = lax.dot_general(
             qs[r], g_ref[...], (((1,), (1,)), ((), ())), preferred_element_type=jnp.float32)
 
-        @pl.loop(0, groups)
+        @pl.loop(0, groups, unroll=2)
         def _(i):
             at = pl.ds(pl.multiple_of(i * GROUP, GROUP), GROUP)
             keys = keys_of(r, i)
@@ -150,7 +150,7 @@
         anchor = jnp.sum(pos_in[r], axis=0)
         cols[r, 0] = jnp.transpose(jnp.concatenate([anchor, anchor], axis=0))
 
-        @pl.loop(0, groups)
+        @pl.loop(0, groups, unroll=2)
         def _(i):
             at = pl.ds(pl.multiple_of(i * GROUP, GROUP), GROUP)
             anchors = cols[r, 0, at, :]
@@ -160,12 +160,11 @@
             for c in range(chunks):
                 s = sc[r, at, c * LANES:(c + 1) * LANES]
                 for m in range(members):
-                    u = 1.0 + jnp.tanh(s - a[m])
-                    total[m] = total[m] + u
-                    square[m] = square[m] + u * u
-            sums = [jnp.sum(x, axis=1, keepdims=True) for x in total]
-            slopes = [
-                jnp.sum(2.0 * x - y, axis=1, keepdims=True) for x, y in zip(total, square)]
+                    t = jnp.tanh(s - a[m])
+                    total[m] = total[m] + t
+                    square[m] = square[m] + t * t
+            sums = [jnp.sum(chunks + x, axis=1, keepdims=True) for x in total]
+            slopes = [jnp.sum(chunks - x, axis=1, keepdims=True) for x in square]
             stage[at, :] = to_lanes(sums + slopes)
 
         rank_in[r, 0] = jnp.transpose(stage[...])[:2 * members]
@@ -199,7 +198,7 @@
         wr = wr / (members * cuts)
         cols[r, 1] = jnp.transpose(jnp.concatenate([wr * (0.25 / TEMP), wr * slope], axis=0))
 
-        @pl.loop(0, groups)
+        @pl.loop(0, groups, unroll=2)
         def _(i):
             at = pl.ds(pl.multiple_of(i * GROUP, GROUP), GROUP)
             at_all = pl.ds(pl.multiple_of(r * rows + i * GROUP, GROUP), GROUP)

time: 139 us -> 108 us (0.78)
  Pallas kernels: 133 us -> 102 us
    pallas_call x1, Pallas kernels: 133 us -> 102 us  [shards(): pl.pallas_call(functools.partial(kernel, n, npb), out_shape=(jax.ShapeDty...]
where the time goes in v3:
time: 108 us
  Pallas kernels  102 us (94%)
  local copies, waits for them, and re-layouts  4.93 us (5%)
    pallas_call x1, Pallas kernels, shards(): pl.pallas_call(functools.partial(kernel, n, npb), out_shape=(jax.ShapeDty...  102 us
    unnamed x5, local copies, waits for them, and re-layouts  4.93 us

profile of v3, /device:TPU:16, one launch (start us, length us, event | category | flops | bytes accessed | tf_op | source)
XLA Modules:
  0.0 107.6 jit_solution(3526807270437950443)
XLA Ops:
  0.6 2.1 %copy.6.idx_ref = s32[2048,4]{1,0:T(8,128)} copy(s32[2048,4]{0,1:T(4,128)} %param.6) | data formatting | bytes 65536 | tf_op args[2]
  2.7 102.0 %shard_map.59 = (f32[256,512]{1,0:T(8,128)}, f32[384,512]{1,0:T(8,128)}) custom-call(s32[4]{0:T(128)} %cut_ref.1, bf16[256,512]{1,0:T(8,128)(2,1)} %q_ref.1, bf16[1536,512]{1,0:T(8,128)(2,1)} %g_ref.1, s32[2048,4]{1,0:T(8,128)} %copy.6.idx_ref), custom_call_target="tpu_custom_call" | custom-call | tf_op jit(solution)/shard_map/pallas_call | solution.py:319
  104.8 0.0 copy-start
  104.8 1.9 %copy.9 = f32[256,512]{1,0:T(8,128)} copy(f32[256,512]{1,0:T(8,128)} %get-tuple-element.4) | data formatting | bytes 1048576
  106.7 0.0 copy-done
  106.7 0.9 copy.10
Async XLA Ops:
  104.8 2.0 %copy-start = (f32[384,512]{1,0:T(8,128)S(1)}, f32[384,512]{1,0:T(8,128)}, u32[]{:S(2)}) copy-start(f32[384,512]{1,0:T(8,128)} %get-tuple-element.5) | copy-start | bytes 2359300

commit v4 on v3

--- a/solution.py
+++ b/solution.py
@@ -116,7 +116,7 @@
         sc[r] = lax.dot_general(
             qs[r], g_ref[...], (((1,), (1,)), ((), ())), preferred_element_type=jnp.float32)
 
-        @pl.loop(0, groups, unroll=2)
+        @pl.loop(0, groups, unroll=min(groups, 4))
         def _(i):
             at = pl.ds(pl.multiple_of(i * GROUP, GROUP), GROUP)
             keys = keys_of(r, i)
@@ -150,7 +150,7 @@
         anchor = jnp.sum(pos_in[r], axis=0)
         cols[r, 0] = jnp.transpose(jnp.concatenate([anchor, anchor], axis=0))
 
-        @pl.loop(0, groups, unroll=2)
+        @pl.loop(0, groups, unroll=min(groups, 4))
         def _(i):
             at = pl.ds(pl.multiple_of(i * GROUP, GROUP), GROUP)
             anchors = cols[r, 0, at, :]
@@ -198,7 +198,7 @@
         wr = wr / (members * cuts)
         cols[r, 1] = jnp.transpose(jnp.concatenate([wr * (0.25 / TEMP), wr * slope], axis=0))
 
-        @pl.loop(0, groups, unroll=2)
+        @pl.loop(0, groups, unroll=min(groups, 4))
         def _(i):
             at = pl.ds(pl.multiple_of(i * GROUP, GROUP), GROUP)
             at_all = pl.ds(pl.multiple_of(r * rows + i * GROUP, GROUP), GROUP)

time: 108 us -> 107 us (level)
    pallas_call x1, Pallas kernels: 102 us -> 101 us  [shards(): pl.pallas_call(functools.partial(kernel, n, npb), out_shape=(jax.ShapeDty...]
where the time goes in v4:
time: 107 us; the launch traced here: 106 us
  Pallas kernels  101 us (94%)
  local copies, waits for them, and re-layouts  4.93 us (5%)
    pallas_call x1, Pallas kernels, shards(): pl.pallas_call(functools.partial(kernel, n, npb), out_shape=(jax.ShapeDty...  101 us
    unnamed x5, local copies, waits for them, and re-layouts  4.93 us

profile of v4, /device:TPU:16, one launch (start us, length us, event | category | flops | bytes accessed | tf_op | source)
XLA Modules:
  0.0 106.4 jit_solution(14279685666064090633)
XLA Ops:
  0.6 2.1 %copy.6.idx_ref = s32[2048,4]{1,0:T(8,128)} copy(s32[2048,4]{0,1:T(4,128)} %param.6) | data formatting | bytes 65536 | tf_op args[2]
  2.7 100.8 %shard_map.59 = (f32[256,512]{1,0:T(8,128)}, f32[384,512]{1,0:T(8,128)}) custom-call(s32[4]{0:T(128)} %cut_ref.1, bf16[256,512]{1,0:T(8,128)(2,1)} %q_ref.1, bf16[1536,512]{1,0:T(8,128)(2,1)} %g_ref.1, s32[2048,4]{1,0:T(8,128)} %copy.6.idx_ref), custom_call_target="tpu_custom_call" | custom-call | tf_op jit(solution)/shard_map/pallas_call | solution.py:319
  103.6 0.0 copy-start
  103.6 1.9 %copy.9 = f32[256,512]{1,0:T(8,128)} copy(f32[256,512]{1,0:T(8,128)} %get-tuple-element.4) | data formatting | bytes 1048576
  105.5 0.0 copy-done
  105.5 0.9 copy.10
Async XLA Ops:
  103.6 2.0 %copy-start = (f32[384,512]{1,0:T(8,128)S(1)}, f32[384,512]{1,0:T(8,128)}, u32[]{:S(2)}) copy-start(f32[384,512]{1,0:T(8,128)} %get-tuple-element.5) | copy-start | bytes 2359300
